TPU v7x, 32 devices: a whole 2x2x4 slice. The times are simulated.
32 devices in a mesh: row: 8 (over z, core), col: 4 (over y, x).
Axes of the slice: x: 2, y: 2, z: 4, core: 2. Of those that a mesh axis runs over, the one named last changes fastest.
Arguments:
- tokens: bfloat16 [16384, 1024], P('row', 'col'), may hold values from -6 to 6
- memory: bfloat16 [4096, 1024], P('row', 'col'), may hold values from -6 to 6
- old_memory: bfloat16 [12288, 1024], P('row', 'col'), may hold values from -6 to 6
- doc_ids: int32 [8, 4096], P('row'), may hold values from 0 to 5, as said below
- norm_gains: bfloat16 [2, 1024], P(None, 'row'), may hold values from 0.5 to 1.5
- comp_weight: bfloat16 [3072, 1024], P('row', 'col'), may hold values from -0.109375 to 0.109375
- query_weight: bfloat16 [1024, 1024], P('row', 'col'), may hold values from -0.1875 to 0.1875
- key_weight: bfloat16 [1024, 1024], P('row', 'col'), may hold values from -0.1875 to 0.1875
- value_weight: bfloat16 [1024, 1024], P('row', 'col'), may hold values from -0.1875 to 0.1875
- proj_weight: bfloat16 [1024, 1024], P('col', 'row'), may hold values from -1.5 to 1.5
- up_weight: bfloat16 [1024, 4096], P('row', 'col'), may hold values from -0.1875 to 0.1875
- down_weight: bfloat16 [4096, 1024], P('col', 'row'), may hold values from -0.09375 to 0.09375
- cotangent: bfloat16 [16384, 1024], P('row', 'col'), may hold values from -6 to 6
Outputs:
- layer_out: bfloat16 [16384, 1024], P('row', 'col')
- grad_x: float32 [16384, 1024], P('row', 'col')
- grad_gains: float32 [2, 1024], P(None, 'row')
- grad_comp: float32 [3072, 1024], P('row', 'col')
- grad_query: float32 [1024, 1024], P('row', 'col')
- grad_key: float32 [1024, 1024], P('row', 'col')
- grad_value: float32 [1024, 1024], P('row', 'col')
- grad_proj: float32 [1024, 1024], P('col', 'row')
- grad_up: float32 [1024, 4096], P('row', 'col')
- grad_down: float32 [4096, 1024], P('col', 'row')
Inputs may be any that keep to these rules, and one draw needn't show every extreme that they name: In each row of doc_ids the numbers never fall and every number occurs; every document covers 200 entries or more.
All inputs are finite; a program needn't handle non-finite values.
Results may differ from a plain program's by a relative error of at most 0.015.
Values may be sent and summed in bfloat16 or wider, within the bound.
A program may use at most 192 MiB of HBM per device.

v0:
```python
import jax
import jax.numpy as jnp
from jax import lax
from jax.sharding import PartitionSpec as P

RATE = 3
HD = 128


def normalize(rows, gain):
    centre = rows - jnp.mean(rows, axis=-1, keepdims=True)
    spread = jnp.mean(centre * centre, axis=-1, keepdims=True)
    return centre * lax.rsqrt(spread + 1e-05) * gain


def contract_rows(left, right):
    return lax.dot_general(
        left, right, (((0,), (0,)), ((), ())), preferred_element_type=jnp.float32
    )


def contract_cols(left, right):
    return lax.dot_general(
        left, right, (((1,), (1,)), ((), ())), preferred_element_type=jnp.float32
    )


def on_device(
    tokens,
    memory,
    old_memory,
    doc_ids,
    norm_gains,
    comp_weight,
    query_weight,
    key_weight,
    value_weight,
    proj_weight,
    up_weight,
    down_weight,
    cotangent,
):
    full_tokens, full_memory, full_old, full_grad = (
        lax.all_gather(tokens, "col", axis=1, tiled=True),
        lax.all_gather(memory, "col", axis=1, tiled=True),
        lax.all_gather(old_memory, "col", axis=1, tiled=True),
        lax.all_gather(cotangent, "col", axis=1, tiled=True),
    )
    comp_full, query_full, key_full, value_full, up_full = (
        lax.all_gather(comp_weight, "row", axis=0, tiled=True),
        lax.all_gather(query_weight, "row", axis=0, tiled=True),
        lax.all_gather(key_weight, "row", axis=0, tiled=True),
        lax.all_gather(value_weight, "row", axis=0, tiled=True),
        lax.all_gather(up_weight, "row", axis=0, tiled=True),
    )
    proj_full, down_full, gain_full = (
        lax.all_gather(proj_weight, "row", axis=1, tiled=True),
        lax.all_gather(down_weight, "row", axis=1, tiled=True),
        lax.all_gather(norm_gains, "row", axis=1, tiled=True),
    )
    width = full_tokens.shape[1]
    slab = tokens.shape[1]
    column = lax.axis_index("col")
    seq_len = tokens.shape[0]
    mem_len = memory.shape[0]
    comp_len = old_memory.shape[0] // RATE
    start_tok = comp_len + mem_len
    all_keys = start_tok + seq_len
    gain_one = gain_full[0].astype(jnp.float32)
    gain_two = gain_full[1].astype(jnp.float32)
    old_rows = full_old.reshape(comp_len, RATE * width)
    compressed = jnp.dot(old_rows, comp_full, preferred_element_type=jnp.float32).astype(
        jnp.bfloat16
    )
    compressed_all = lax.all_gather(compressed, "col", axis=1, tiled=True)
    stacked = jnp.concatenate([compressed_all, full_memory, full_tokens], axis=0).astype(
        jnp.float32
    )
    normed = normalize(stacked, gain_one).astype(jnp.bfloat16)
    queries = jnp.dot(normed[start_tok:], query_full, preferred_element_type=jnp.float32).astype(
        jnp.bfloat16
    )
    keys = jnp.dot(normed, key_full, preferred_element_type=jnp.float32).astype(jnp.bfloat16)
    values = jnp.dot(normed, value_full, preferred_element_type=jnp.float32).astype(jnp.bfloat16)
    local_heads = queries.shape[1] // HD
    key_heads = keys.reshape(all_keys, local_heads, HD)
    value_heads = values.reshape(all_keys, local_heads, HD)
    doc_row = doc_ids[0]
    key_doc = jnp.concatenate(
        [doc_row[RATE - 1 : RATE * comp_len : RATE], doc_row[RATE * comp_len :]]
    )
    key_place = jnp.arange(all_keys, dtype=jnp.int32) - start_tok
    query_doc = doc_row[RATE * comp_len + mem_len :]
    query_place = jnp.arange(seq_len, dtype=jnp.int32)
    block = min(512, seq_len)
    steps_count = seq_len // block
    scale = HD ** (-0.5)
    query_blocks = queries.reshape(steps_count, block, local_heads, HD)
    doc_blocks = query_doc.reshape(steps_count, block)
    place_blocks = query_place.reshape(steps_count, block)

    def masked_scores(query_block, doc_block, place_block):
        allowed = (doc_block[:, None] == key_doc[None, :]) & (
            key_place[None, :] <= place_block[:, None]
        )
        scores = (
            jnp.einsum("qhd,khd->hqk", query_block, key_heads, preferred_element_type=jnp.float32)
            * scale
        )
        return jnp.where(allowed[None], scores, -1e30)

    def forward_block(items):
        query_block, doc_block, place_block = items
        scores = masked_scores(query_block, doc_block, place_block)
        top = jnp.max(scores, axis=-1, keepdims=True)
        raw = jnp.exp(scores - top)
        total = jnp.sum(raw, axis=-1, keepdims=True)
        rounded = (raw / total).astype(jnp.bfloat16)
        mixed_block = jnp.einsum(
            "hqk,khd->qhd", rounded, value_heads, preferred_element_type=jnp.float32
        )
        return (mixed_block, top, total)

    mixed_blocks, tops, totals = lax.map(forward_block, (query_blocks, doc_blocks, place_blocks))
    mixed = mixed_blocks.reshape(seq_len, local_heads * HD).astype(jnp.bfloat16)
    branch = lax.psum(jnp.dot(mixed, proj_full, preferred_element_type=jnp.float32), "col")
    resid = full_tokens.astype(jnp.float32) + branch
    hidden_in = normalize(resid, gain_two).astype(jnp.bfloat16)
    upper = jnp.dot(hidden_in, up_full, preferred_element_type=jnp.float32)
    active = jax.nn.gelu(upper).astype(jnp.bfloat16)
    down_terms = jnp.dot(active, down_full, preferred_element_type=jnp.float32)
    final = resid + lax.psum(down_terms.astype(jnp.bfloat16), "col").astype(jnp.float32)
    layer_out = lax.dynamic_slice_in_dim(final, column * slab, slab, 1).astype(jnp.bfloat16)
    grad_down = contract_rows(active, full_grad)
    grad_active = contract_cols(full_grad, down_full)
    _, gelu_pull = jax.vjp(jax.nn.gelu, upper)
    grad_upper = gelu_pull(grad_active)[0].astype(jnp.bfloat16)
    grad_up = contract_rows(hidden_in, grad_upper)
    grad_hidden = lax.psum(contract_cols(grad_upper, up_full), "col")
    _, second_pull = jax.vjp(normalize, resid, gain_two)
    grad_resid_norm, grad_gain_two = second_pull(grad_hidden)
    grad_resid = full_grad.astype(jnp.float32) + grad_resid_norm
    grad_branch = grad_resid.astype(jnp.bfloat16)
    grad_proj = contract_rows(mixed, grad_branch)
    grad_mixed = contract_cols(grad_branch, proj_full).astype(jnp.bfloat16)
    grad_blocks = grad_mixed.reshape(steps_count, block, local_heads, HD)

    def backward_block(carry, items):
        grad_keys, grad_values = carry
        query_block, doc_block, place_block, top, total, grad_out = items
        scores = masked_scores(query_block, doc_block, place_block)
        probs = jnp.exp(scores - top) / total
        rounded = probs.astype(jnp.bfloat16)
        grad_probs = jnp.einsum(
            "qhd,khd->hqk", grad_out, value_heads, preferred_element_type=jnp.float32
        )
        grad_scores = (
            probs * (grad_probs - jnp.sum(probs * grad_probs, axis=-1, keepdims=True))
        ).astype(jnp.bfloat16)
        grad_query_block = (
            jnp.einsum("hqk,khd->qhd", grad_scores, key_heads, preferred_element_type=jnp.float32)
            * scale
        )
        grad_keys = (
            grad_keys
            + jnp.einsum(
                "hqk,qhd->khd", grad_scores, query_block, preferred_element_type=jnp.float32
            )
            * scale
        )
        grad_values = grad_values + jnp.einsum(
            "hqk,qhd->khd", rounded, grad_out, preferred_element_type=jnp.float32
        )
        return ((grad_keys, grad_values), grad_query_block)

    empty = jnp.zeros((all_keys, local_heads, HD), jnp.float32)
    (grad_key_heads, grad_value_heads), grad_query_blocks = lax.scan(
        backward_block,
        (empty, empty),
        (query_blocks, doc_blocks, place_blocks, tops, totals, grad_blocks),
    )
    grad_queries = grad_query_blocks.reshape(seq_len, local_heads * HD).astype(jnp.bfloat16)
    grad_keys_low = grad_key_heads.reshape(all_keys, local_heads * HD).astype(jnp.bfloat16)
    grad_values_low = grad_value_heads.reshape(all_keys, local_heads * HD).astype(jnp.bfloat16)
    grad_query = contract_rows(normed[start_tok:], grad_queries)
    grad_key = contract_rows(normed, grad_keys_low)
    grad_value = contract_rows(normed, grad_values_low)
    back_keys = contract_cols(grad_keys_low, key_full) + contract_cols(grad_values_low, value_full)
    back_queries = contract_cols(grad_queries, query_full)
    partial_rows = jnp.concatenate(
        [back_keys[:start_tok], back_keys[start_tok:] + back_queries], axis=0
    )
    grad_normed = lax.psum(partial_rows, "col")
    _, first_pull = jax.vjp(normalize, stacked, gain_one)
    grad_stacked, grad_gain_one = first_pull(grad_normed)
    grad_comp_slab = lax.dynamic_slice_in_dim(grad_stacked[:comp_len], column * slab, slab, 1)
    grad_tok_slab = lax.dynamic_slice_in_dim(grad_stacked[start_tok:], column * slab, slab, 1)
    grad_x = lax.dynamic_slice_in_dim(grad_resid, column * slab, slab, 1) + grad_tok_slab
    grad_comp_low = grad_comp_slab.astype(jnp.bfloat16)
    grad_comp = contract_rows(old_rows, grad_comp_low)
    grad_gains = jnp.stack([grad_gain_one, grad_gain_two], axis=0)
    comp_part, query_part, key_part, value_part, up_part = (
        lax.psum_scatter(grad_comp, "row", scatter_dimension=0, tiled=True),
        lax.psum_scatter(grad_query, "row", scatter_dimension=0, tiled=True),
        lax.psum_scatter(grad_key, "row", scatter_dimension=0, tiled=True),
        lax.psum_scatter(grad_value, "row", scatter_dimension=0, tiled=True),
        lax.psum_scatter(grad_up, "row", scatter_dimension=0, tiled=True),
    )
    proj_part, down_part, gains_part = (
        lax.psum_scatter(grad_proj, "row", scatter_dimension=1, tiled=True),
        lax.psum_scatter(grad_down, "row", scatter_dimension=1, tiled=True),
        lax.psum_scatter(grad_gains, "row", scatter_dimension=1, tiled=True),
    )
    return (
        layer_out,
        grad_x,
        gains_part,
        comp_part,
        query_part,
        key_part,
        value_part,
        proj_part,
        up_part,
        down_part,
    )


def solution(mesh):
    in_specs = (
        P("row", "col"),
        P("row", "col"),
        P("row", "col"),
        P("row", None),
        P(None, "row"),
        P("row", "col"),
        P("row", "col"),
        P("row", "col"),
        P("row", "col"),
        P("col", "row"),
        P("row", "col"),
        P("col", "row"),
        P("row", "col"),
    )
    out_specs = (
        P("row", "col"),
        P("row", "col"),
        P(None, "row"),
        P("row", "col"),
        P("row", "col"),
        P("row", "col"),
        P("row", "col"),
        P("col", "row"),
        P("row", "col"),
        P("col", "row"),
    )
    return jax.shard_map(
        on_device, mesh=mesh, in_specs=in_specs, out_specs=out_specs, check_vma=False
    )
```

profile of v0, /device:TPU:0, one launch (start us, length us, event | category | flops | bytes accessed | tf_op | source)
XLA Modules:
  0.0 1541.5 jit_solution(4942058512463735601)
XLA Ops:
  10.1 46.2 %all-gather.11.cloned.1.call-done = bf16[1536,1024]{1,0:T(8,128)(2,1)} async-done(((bf16[1536,256]{1,0:T(8,128)(2,1)}), bf16[1536,1024]{1,0:T(8,128)(2,1)}) %all-gather.11.cloned.1.call-update) | async-done | bytes 3145744 | tf_op jit(solution)/shard_map/all_gather | solution.py:46
  60.6 22.7 %all-gather.13.cloned.1.call-done = bf16[3072,256]{1,0:T(8,128)(2,1)} async-done(((bf16[384,256]{1,0:T(8,128)(2,1)}), bf16[3072,256]{1,0:T(8,128)(2,1)}) %all-gather.13.cloned.1.call-update) | async-done | bytes 1572880 | tf_op jit(solution)/shard_map/all_gather | solution.py:50
  88.0 9.9 all_gather.44
  98.6 15.8 %all_gather.45 = bf16[1024,256]{1,0:T(8,128)(2,1)} all-gather(bf16[128,256]{1,0:T(8,128)(2,1)S(1)} %copy-done.47), channel_id=1, replica_groups=mesh['row'=8,'col'=4] {'row'}, dimensions={0}, use_global_device_ids=true | all-gather | bytes 589824 | tf_op jit(solution)/shard_map/all_gather | solution.py:51
  114.4 15.8 %all_gather.46 = bf16[1024,256]{1,0:T(8,128)(2,1)} all-gather(bf16[128,256]{1,0:T(8,128)(2,1)S(1)} %copy-done.48), channel_id=1, replica_groups=mesh['row'=8,'col'=4] {'row'}, dimensions={0}, use_global_device_ids=true | all-gather | bytes 589824 | tf_op jit(solution)/shard_map/all_gather | solution.py:52
  130.2 15.8 %all_gather.47 = bf16[1024,256]{1,0:T(8,128)(2,1)} all-gather(bf16[128,256]{1,0:T(8,128)(2,1)S(1)} %copy-done.49), channel_id=1, replica_groups=mesh['row'=8,'col'=4] {'row'}, dimensions={0}, use_global_device_ids=true | all-gather | bytes 589824 | tf_op jit(solution)/shard_map/all_gather | solution.py:53
  146.1 15.2 all_gather.48
  164.8 28.6 %all-gather.15.cloned.1.call-done = bf16[512,1024]{1,0:T(8,128)(2,1)} async-done(((bf16[512,256]{1,0:T(8,128)(2,1)}), bf16[512,1024]{1,0:T(8,128)(2,1)}) %all-gather.15.cloned.1.call-update) | async-done | bytes 1048592 | tf_op jit(solution)/shard_map/all_gather | solution.py:75
  197.5 6.0 fusion.42
  204.1 5.9 fusion.40
  215.3 5.9 convolution_convert_fusion
  223.1 5.8 convolution_convert_fusion.1
  232.0 61.1 %while.30 = (s32[]{:T(128)}, bf16[4,512,2,128]{3,1,2,0:T(8,128)(2,1)}, f32[4,2,512,1]{2,1,3,0:T(2,128)S(1)}, f32[4,2,512,1]{2,1,3,0:T(2,128)S(1)}, s32[4,512]{1,...) while((s32[]{:T(128)}, ...), condition=%wide.region_5.6_spmd.clone, body=%wide.region_2.5_spmd.clone.sunk | while | flops 1653081088 | bytes 56447168 | solution.py:124
  241.6 4.8 fusion.140
  256.8 4.8 fusion.140
  272.0 4.8 fusion.140
  287.3 4.8 fusion.140
  297.2 5.6 fusion.65
  303.6 10.7 fusion.78
  314.3 160.6 %all-reduce.5.cloned.1.call-done = f32[2048,1024]{1,0:T(8,128)} async-done(((f32[2048,1024]{1,0:T(8,128)}), f32[2048,1024]{1,0:T(8,128)}) %all-reduce.5.cloned.1.call-update) | async-done | bytes 8388624 | tf_op jit(solution)/shard_map/psum | solution.py:126
  474.9 5.5 fusion.77
  486.3 20.1 %all-gather.19.cloned.1.call-done = bf16[1024,1024]{1,0:T(8,128)(2,1)} async-done(((bf16[128,1024]{1,0:T(8,128)(2,1)}), bf16[1024,1024]{1,0:T(8,128)(2,1)}) %all-gather.19.cloned.1.call-update) | async-done | bytes 2097168 | tf_op jit(solution)/shard_map/all_gather | solution.py:54
  506.4 16.1 %fusion.50 = (bf16[2048,1024]{1,0:T(8,128)(2,1)S(1)}, f32[2048,1024]{1,0:T(8,128)}) fusion(f32[2048,1024]{1,0:T(8,128)} %fusion.78, bf16[2048,1024]{1,0:T(8,128)(2,1)} %multiply_convert_fusion.2, bf16[1024,1024]{1,0:T(8,128)(2,1)} %all-gather.19.cloned.1.call-done), kind=kOutput, calls=%fused_computation.73 | convolution fusion | flops 4336910336 | bytes 27262976 | tf_op jit(solution)/shard_map/dot_general | solution.py:129
  524.5 7.0 fusion.79
  531.6 171.5 %all-reduce.9.cloned.1.call-done = f32[2048,1024]{1,0:T(8,128)} async-done(((f32[2048,1024]{1,0:T(8,128)}), f32[2048,1024]{1,0:T(8,128)}) %all-reduce.9.cloned.1.call-update) | async-done | bytes 8388624 | tf_op jit(solution)/shard_map/psum | solution.py:139
  703.1 8.2 multiply_reduce_fusion.1
  711.4 5.0 fusion.76
  726.2 122.1 %while.31 = (s32[]{:T(128)}, f32[3072,2,128]{0,2,1:T(8,128)S(1)}, f32[3072,2,128]{0,2,1:T(8,128)}, bf16[4,512,2,128]{3,1,2,0:T(8,128)(2,1)}, bf16[4,512,2,128]{3...) while((s32[]{:T(128)}, f32[3072,2,128]{0,2,1:T(8,128)S(1)}, ...), condition=%wide.region_15.16_spmd.clone, body=%wide.region_13.15_spmd.clone.sunk | while | flops 4066772992 | bytes 161038704 | solution.py:177
  729.1 7.8 fusion.148
  736.9 8.3 multiply_reduce_fusion.5
  745.2 5.7 multiply_convert_fusion.6
  759.6 7.8 fusion.148
  767.4 8.3 multiply_reduce_fusion.5
  775.7 5.7 multiply_convert_fusion.6
  790.1 7.8 fusion.148
  797.9 8.3 multiply_reduce_fusion.5
  806.2 5.7 multiply_convert_fusion.6
  820.6 7.8 fusion.148
  828.4 8.3 multiply_reduce_fusion.5
  836.7 5.7 multiply_convert_fusion.6
  858.8 4.6 slice_add_fusion
  863.4 11.9 pad_maximum_fusion
  875.6 11.8 convolution_convert_fusion.2
  887.5 227.9 %all-reduce.11.cloned.1.call-done = f32[3072,1024]{1,0:T(8,128)} async-done(((f32[3072,1024]{1,0:T(8,128)}), f32[3072,1024]{1,0:T(8,128)}) %all-reduce.11.cloned.1.call-update) | async-done | bytes 12582928 | tf_op jit(solution)/shard_map/psum | solution.py:193
  1115.5 9.9 fusion.43
  1126.9 11.9 fusion.41
  1139.9 11.5 broadcast_add_fusion
  1151.4 4.9 copy-done.11
  1156.5 4.5 convolution_bitcast_fusion
  1161.4 10.2 fusion.83
  1171.6 12.3 fusion.74
  1184.0 5.6 fusion.59
  1189.7 4.9 fusion.51
  1195.1 6.1 fusion.81
  1201.3 5.6 fusion.82
  1206.9 15.3 all-reduce.7.cloned.1.call-done
  1232.0 23.9 %reduce-scatter.25.cloned.1.call-done = f32[128,2]{1,0:T(8,128)} async-done(((f32[1024,2]{1,0:T(8,128)}), f32[128,2]{1,0:T(8,128)}) %reduce-scatter.25.cloned.1.call-update) | async-done | bytes 1040
  1257.4 39.2 %reduce-scatter.11.cloned.1.call-done = f32[384,256]{0,1:T(8,128)} async-done(((f32[3072,256]{0,1:T(8,128)}), f32[384,256]{0,1:T(8,128)}) %reduce-scatter.11.cloned.1.call-update) | async-done | bytes 393232 | tf_op jit(solution)/shard_map/reduce_scatter | solution.py:203
  1298.6 50.2 %reduce-scatter.21.cloned.1.call-done = f32[128,1024]{1,0:T(8,128)} async-done(((f32[1024,1024]{1,0:T(8,128)}), f32[128,1024]{1,0:T(8,128)}) %reduce-scatter.21.cloned.1.call-update) | async-done | bytes 524304 | tf_op jit(solution)/shard_map/reduce_scatter | solution.py:207
  1348.7 51.1 %reduce-scatter.23.cloned.1.call-done = f32[1024,128]{1,0:T(8,128)} async-done(((f32[1024,1024]{1,0:T(8,128)}), f32[1024,128]{1,0:T(8,128)}) %reduce-scatter.23.cloned.1.call-update) | async-done | bytes 524304 | tf_op jit(solution)/shard_map/reduce_scatter | solution.py:211
  1399.8 33.8 %reduce-scatter.19.cloned.1.call-done = f32[256,128]{1,0:T(8,128)} async-done(((f32[256,1024]{1,0:T(8,128)}), f32[256,128]{1,0:T(8,128)}) %reduce-scatter.19.cloned.1.call-update) | async-done | bytes 131088 | tf_op jit(solution)/shard_map/reduce_scatter | solution.py:210
  1433.7 33.6 %reduce-scatter.13.cloned.1.call-done = f32[128,256]{1,0:T(8,128)} async-done(((f32[1024,256]{1,0:T(8,128)}), f32[128,256]{1,0:T(8,128)}) %reduce-scatter.13.cloned.1.call-update) | async-done | bytes 131088 | tf_op jit(solution)/shard_map/reduce_scatter | solution.py:204
  1467.2 33.8 %reduce-scatter.15.cloned.1.call-done = f32[128,256]{1,0:T(8,128)} async-done(((f32[1024,256]{1,0:T(8,128)}), f32[128,256]{1,0:T(8,128)}) %reduce-scatter.15.cloned.1.call-update) | async-done | bytes 131088 | tf_op jit(solution)/shard_map/reduce_scatter | solution.py:205
  1501.0 33.5 %reduce-scatter.17.cloned.1.call-done = f32[128,256]{1,0:T(8,128)} async-done(((f32[1024,256]{1,0:T(8,128)}), f32[128,256]{1,0:T(8,128)}) %reduce-scatter.17.cloned.1.call-update) | async-done | bytes 131088 | tf_op jit(solution)/shard_map/reduce_scatter | solution.py:206
  (315 shorter events, 156.4 us)
Async XLA Ops:
  7.2 80.6 %copy-start.52 = (s32[1,4096]{1,0:T(1,128)S(1)}, s32[1,4096]{1,0:T(1,128)}, u32[]{:S(2)}) copy-start(s32[1,4096]{1,0:T(1,128)} %param.20) | copy-start | bytes 49156
  7.2 80.8 %copy-start.54 = (bf16[2,128]{1,0:T(2,128)(2,1)S(1)}, bf16[2,128]{1,0:T(2,128)(2,1)}, u32[]{:S(2)}) copy-start(bf16[2,128]{1,0:T(2,128)(2,1)} %param.21) | copy-start | bytes 1540
  7.2 91.4 %copy-start.47 = (bf16[128,256]{1,0:T(8,128)(2,1)S(1)}, bf16[128,256]{1,0:T(8,128)(2,1)}, u32[]{:S(2)}) copy-start(bf16[128,256]{1,0:T(8,128)(2,1)} %param.23) | copy-start | bytes 196612
  7.2 107.2 %copy-start.48 = (bf16[128,256]{1,0:T(8,128)(2,1)S(1)}, bf16[128,256]{1,0:T(8,128)(2,1)}, u32[]{:S(2)}) copy-start(bf16[128,256]{1,0:T(8,128)(2,1)} %param.24) | copy-start | bytes 196612
  7.2 49.1 %all-gather.11.cloned.1.call-start = ((), (), s32[]{:S(2)}) async-start(), calls=%async_computation.9 | async-start | bytes 3932160 | tf_op jit(solution)/shard_map/all_gather | solution.py:46
  8.0 122.3 %copy-start.49 = (bf16[128,256]{1,0:T(8,128)(2,1)S(1)}, bf16[128,256]{1,0:T(8,128)(2,1)}, u32[]{:S(2)}) copy-start(bf16[128,256]{1,0:T(8,128)(2,1)} %param.25) | copy-start | bytes 196612
  8.0 75.3 %all-gather.13.cloned.1.call-start = ((), (), s32[]{:S(2)}) async-start(), calls=%async_computation.10 | async-start | bytes 1769472 | tf_op jit(solution)/shard_map/all_gather | solution.py:50
  8.7 152.6 %all-gather.17.cloned.1.call-start = ((), (), s32[]{:S(2)}) async-start(), calls=%async_computation.12 | async-start | bytes 1310720 | tf_op jit(solution)/shard_map/all_gather | solution.py:45
  9.4 136.6 %copy-start.50 = (bf16[256,128]{1,0:T(8,128)(2,1)S(1)}, bf16[256,128]{1,0:T(8,128)(2,1)}, u32[]{:S(2)}) copy-start(bf16[256,128]{1,0:T(8,128)(2,1)} %param.26) | copy-start | bytes 196612
  9.5 155.3 %all-gather.9.cloned.1.call-start = ((), (), s32[]{:S(2)}) async-start(), calls=%async_computation.8 | async-start | bytes 5242880 | tf_op jit(solution)/shard_map/all_gather | solution.py:44
  10.0 183.4 %all-gather.15.cloned.1.call-start = ((), (), s32[]{:S(2)}) async-start(), calls=%async_computation.11 | async-start | bytes 1310720 | tf_op jit(solution)/shard_map/all_gather | solution.py:75
  60.5 100.8 %copy-start.19 = (bf16[512,3072]{1,0:T(8,128)(2,1)}, bf16[512,3072]{1,0:T(8,128)(2,1)S(1)}, u32[]{:S(2)}) copy-start(bf16[512,3072]{1,0:T(8,128)(2,1)S(1)} %reshape.251) | copy-start | bytes 9437188
  86.4 217.2 %all-gather.21.cloned.1.call-start = ((), (), s32[]{:S(2)}) async-start(), calls=%async_computation.15 | async-start | bytes 2359296 | tf_op jit(solution)/shard_map/all_gather | solution.py:58
  86.9 216.6 %all-gather.23.cloned.1.call-start = ((), (), s32[]{:S(2)}) async-start(), calls=%async_computation.17 | async-start | bytes 5242880 | tf_op jit(solution)/shard_map/all_gather | solution.py:47
  87.7 387.2 %all-reduce.5.cloned.1.call-start = ((), (), s32[]{:S(2)}) async-start(), calls=%async_computation.13 | async-start | bytes 16777216 | tf_op jit(solution)/shard_map/psum | solution.py:126
  98.5 111.4 %copy-start.45 = (f32[1,1024]{1,0:T(1,128)}, f32[1,1024]{1,0:T(1,128)S(1)}, u32[]{:S(2)}) copy-start(f32[1,1024]{1,0:T(1,128)S(1)} %get-tuple-element.379) | copy-start | bytes 12292
  161.3 42.7 %copy-start.12 = (bf16[512,1024]{1,0:T(8,128)(2,1)S(1)}, bf16[512,1024]{1,0:T(8,128)(2,1)}, u32[]{:S(2)}) copy-start(bf16[512,1024]{1,0:T(8,128)(2,1)} %all-gather.17.cloned.1.call-done) | copy-start | bytes 3145732
  193.4 10.7 copy-start.14
  197.5 6.0 copy-start.39
  197.5 15.1 copy-start.35
  215.3 7.8 copy-start.37
  293.1 9.6 copy-start.8
  293.1 9.6 copy-start.9
  302.8 203.6 %all-gather.19.cloned.1.call-start = ((), (), s32[]{:S(2)}) async-start(), calls=%async_computation.14 | async-start | bytes 2359296 | tf_op jit(solution)/shard_map/all_gather | solution.py:54
  303.5 399.6 %all-reduce.9.cloned.1.call-start = ((), (), s32[]{:S(2)}) async-start(), calls=%async_computation.18 | async-start | bytes 16777216 | tf_op jit(solution)/shard_map/psum | solution.py:139
  506.4 18.2 %copy-start.55 = (bf16[1024,1024]{1,0:T(8,128)(2,1)S(1)}, bf16[1024,1024]{1,0:T(8,128)(2,1)}, u32[]{:S(2)}) copy-start(bf16[1024,1024]{1,0:T(8,128)(2,1)} %all-gather.19.cloned.1.call-done) | copy-start | bytes 6291460
  531.5 583.9 %all-reduce.11.cloned.1.call-start = ((), (), s32[]{:S(2)}) async-start(), calls=%async_computation.19 | async-start | bytes 25165824 | tf_op jit(solution)/shard_map/psum | solution.py:193
  703.1 8.2 copy-start.16
  711.4 5.0 copy-start.27
  716.4 4.3 copy-start.26
  726.2 10.7 copy-start.10
  726.2 10.7 copy-start.25
  745.2 5.7 copy-start.5
  756.7 10.7 copy-start.10
  756.7 10.7 copy-start.25
  775.7 5.7 copy-start.5
  787.2 10.7 copy-start.10
  787.2 10.7 copy-start.25
  806.2 5.7 copy-start.5
  817.7 10.7 copy-start.10
  817.7 10.7 copy-start.25
  836.7 5.7 copy-start.5
  875.3 346.9 %all-reduce.7.cloned.1.call-start = ((), (), s32[]{:S(2)}) async-start(), calls=%async_computation.16 | async-start | bytes 8388608 | tf_op jit(solution)/shard_map/psum | solution.py:132
  875.6 239.9 %copy-start.13 = (bf16[512,1024]{1,0:T(8,128)(2,1)S(1)}, bf16[512,1024]{1,0:T(8,128)(2,1)}, u32[]{:S(2)}) copy-start(bf16[512,1024]{1,0:T(8,128)(2,1)} %all-gather.17.cloned.1.call-done) | copy-start | bytes 3145732
  875.6 239.9 %copy-start.15 = (bf16[512,1024]{1,0:T(8,128)(2,1)S(1)}, bf16[512,1024]{1,0:T(8,128)(2,1)}, u32[]{:S(2)}) copy-start(bf16[512,1024]{1,0:T(8,128)(2,1)} %all-gather.15.cloned.1.call-done) | copy-start | bytes 3145732
  875.6 239.9 %copy-start.40 = (f32[3072]{0:T(1024)S(1)}, f32[3072]{0:T(1024)}, u32[]{:S(2)}) copy-start(f32[3072]{0:T(1024)} %copy-done.39) | copy-start | bytes 36868
  875.6 239.9 %copy-start.46 = (f32[1,1024]{1,0:T(1,128)S(1)}, f32[1,1024]{1,0:T(1,128)}, u32[]{:S(2)}) copy-start(f32[1,1024]{1,0:T(1,128)} %copy-done.45) | copy-start | bytes 12292
  887.4 238.0 %copy-start.44 = (f32[3072]{0:T(1024)S(1)}, f32[3072]{0:T(1024)}, u32[]{:S(2)}) copy-start(f32[3072]{0:T(1024)} %copy-done.43) | copy-start | bytes 36868
  887.4 238.0 %copy-start.42 = (f32[3072]{0:T(1024)S(1)}, f32[3072]{0:T(1024)}, u32[]{:S(2)}) copy-start(f32[3072]{0:T(1024)} %copy-done.41) | copy-start | bytes 36868
  887.5 368.5 %reduce-scatter.25.cloned.1.call-start = ((), (), s32[]{:S(2)}) async-start(), calls=%async_computation.27 | async-start | bytes 589824
  1115.4 10.0 copy-start.2
  1115.5 11.5 copy-start.4
  1126.9 11.9 copy-start.53
  1151.4 4.9 copy-start.11
  1156.4 140.2 %reduce-scatter.11.cloned.1.call-start = ((), (), s32[]{:S(2)}) async-start(), calls=%async_computation.20 | async-start | bytes 3538944 | tf_op jit(solution)/shard_map/reduce_scatter | solution.py:203
  1161.1 187.7 %reduce-scatter.21.cloned.1.call-start = ((), (), s32[]{:S(2)}) async-start(), calls=%async_computation.25 | async-start | bytes 4718592 | tf_op jit(solution)/shard_map/reduce_scatter | solution.py:207
  1171.6 12.4 copy-start.21
  1171.6 228.3 %reduce-scatter.23.cloned.1.call-start = ((), (), s32[]{:S(2)}) async-start(), calls=%async_computation.26 | async-start | bytes 4718592 | tf_op jit(solution)/shard_map/reduce_scatter | solution.py:211
  1183.9 249.7 %reduce-scatter.19.cloned.1.call-start = ((), (), s32[]{:S(2)}) async-start(), calls=%async_computation.24 | async-start | bytes 1179648 | tf_op jit(solution)/shard_map/reduce_scatter | solution.py:210
  1189.6 5.5 copy-start.23
  1189.6 277.6 %reduce-scatter.13.cloned.1.call-start = ((), (), s32[]{:S(2)}) async-start(), calls=%async_computation.21 | async-start | bytes 1179648 | tf_op jit(solution)/shard_map/reduce_scatter | solution.py:204
  1194.5 6.7 copy-start.18
  1194.6 306.4 %reduce-scatter.15.cloned.1.call-start = ((), (), s32[]{:S(2)}) async-start(), calls=%async_computation.22 | async-start | bytes 1179648 | tf_op jit(solution)/shard_map/reduce_scatter | solution.py:205
  1201.2 333.3 %reduce-scatter.17.cloned.1.call-start = ((), (), s32[]{:S(2)}) async-start(), calls=%async_computation.23 | async-start | bytes 1179648 | tf_op jit(solution)/shard_map/reduce_scatter | solution.py:206
  (38 other events, 96.0 us)
Sparse Core Ops, SparseCore 0:
  9.8 46.4 all-gather.10
  58.0 25.2 all-gather.12
  85.1 25.4 all-gather.16
  112.3 52.4 all-gather.8
  167.0 26.3 all-gather.14
  194.9 30.5 all-gather.20
  227.3 51.4 all-gather.22
  302.9 171.9 all-reduce.4
  476.5 29.8 all-gather.18
  531.6 171.4 all-reduce.8
  875.4 239.9 all-reduce.10
  1118.6 103.6 all-reduce.6
  1224.5 31.3 reduce-scatter.24
  1258.1 38.5 reduce-scatter.10
  1299.4 49.3 reduce-scatter.20
  1351.4 48.3 reduce-scatter.22
  1402.5 31.0 reduce-scatter.18
  1436.4 30.8 reduce-scatter.12
  1470.1 30.8 reduce-scatter.14
  1503.7 30.7 reduce-scatter.16
where the time goes:
time: 1550 us; the launch traced here: 1540 us
  waiting for transfers between devices  1000 us (65%)
  matrix products  250 us (16%)
  other arithmetic  142 us (9%)
  blocking collectives  72.7 us (5%)
  local copies, waits for them, and re-layouts  58.5 us (4%)
    psum x1, waiting for transfers between devices, on_device(): grad_normed = lax.psum(partial_rows, 'col')  228 us
    psum x1, waiting for transfers between devices, on_device(): grad_hidden = lax.psum(contract_cols(grad_upper, up_full), 'col')  172 us
    psum x1, waiting for transfers between devices, on_device(): lax.psum(jnp.dot(mixed, proj_full, preferred_element_type=jnp.float32), '...  161 us
    reduce_scatter x1, waiting for transfers between devices, on_device(): lax.psum_scatter(grad_down, 'row', scatter_dimension=1, tiled=True)  51.1 us
    reduce_scatter x1, waiting for transfers between devices, on_device(): lax.psum_scatter(grad_up, 'row', scatter_dimension=0, tiled=True)  50.2 us
    dot_general x8, matrix products, masked_scores(): jnp.einsum('qhd,khd->hqk', query_block, key_heads, preferred_element_type...  49.4 us
    dot_general x7, matrix products, contract_rows(): lax.dot_general(left, right, (((0,), (0,)), ((), ())), preferred_element_...  49.2 us
    all_gather x1, waiting for transfers between devices, on_device(): lax.all_gather(old_memory, 'col', axis=1, tiled=True)  46.2 us
  transfers between devices with their start and end apart: 20, of which 17 were waited for; matrix products, arithmetic and copies ran while one was open for 15% of the time, Pallas kernels for 0%

commit v1 on v0

--- a/solution.py
+++ b/solution.py
@@ -190,7 +190,7 @@
     partial_rows = jnp.concatenate(
         [back_keys[:start_tok], back_keys[start_tok:] + back_queries], axis=0
     )
-    grad_normed = lax.psum(partial_rows, "col")
+    grad_normed = jnp.sum(lax.all_gather(partial_rows, "col"), axis=0)
     _, first_pull = jax.vjp(normalize, stacked, gain_one)
     grad_stacked, grad_gain_one = first_pull(grad_normed)
     grad_comp_slab = lax.dynamic_slice_in_dim(grad_stacked[:comp_len], column * slab, slab, 1)

time: 1550 us -> 1740 us (1.12)
  waiting for transfers between devices: 1000 us -> 1170 us
  other arithmetic: 142 us -> 167 us
    all_gather x0 -> x1, waiting for transfers between devices: none -> 424 us  [on_device(): grad_normed = jnp.sum(lax.all_gather(partial_rows, 'col'), axis=0)]
    psum x1 -> x0, waiting for transfers between devices: 228 us -> none  [on_device(): grad_normed = lax.psum(partial_rows, 'col')]
    reduce_sum x0 -> x1, other arithmetic: none -> 24.8 us  [on_device(): grad_normed = jnp.sum(lax.all_gather(partial_rows, 'col'), axis=0)]
  transfers between devices with their start and end apart: 20 -> 20, of which waited for: 17 -> 16; matrix products, arithmetic and copies ran while one was open for 15% -> 15% of each run, Pallas kernels for 0% -> 0%
where the time goes in v1:
time: 1740 us
  waiting for transfers between devices  1170 us (67%)
  matrix products  250 us (14%)
  other arithmetic  167 us (10%)
  blocking collectives  72.7 us (4%)
  local copies, waits for them, and re-layouts  59.3 us (3%)
    all_gather x1, waiting for transfers between devices, on_device(): grad_normed = jnp.sum(lax.all_gather(partial_rows, 'col'), axis=0)  424 us
    psum x1, waiting for transfers between devices, on_device(): grad_hidden = lax.psum(contract_cols(grad_upper, up_full), 'col')  172 us
    psum x1, waiting for transfers between devices, on_device(): lax.psum(jnp.dot(mixed, proj_full, preferred_element_type=jnp.float32), '...  161 us
    reduce_scatter x1, waiting for transfers between devices, on_device(): lax.psum_scatter(grad_down, 'row', scatter_dimension=1, tiled=True)  51.1 us
    reduce_scatter x1, waiting for transfers between devices, on_device(): lax.psum_scatter(grad_up, 'row', scatter_dimension=0, tiled=True)  50 us
    dot_general x7, matrix products, contract_rows(): lax.dot_general(left, right, (((0,), (0,)), ((), ())), preferred_element_...  49.5 us
    dot_general x8, matrix products, masked_scores(): jnp.einsum('qhd,khd->hqk', query_block, key_heads, preferred_element_type...  49.3 us
    all_gather x1, waiting for transfers between devices, on_device(): lax.all_gather(old_memory, 'col', axis=1, tiled=True)  46.2 us
  transfers between devices with their start and end apart: 20, of which 16 were waited for; matrix products, arithmetic and copies ran while one was open for 15% of the time, Pallas kernels for 0%

profile of v1, /device:TPU:0, one launch (start us, length us, event | category | flops | bytes accessed | tf_op | source)
XLA Modules:
  0.0 1738.3 jit_solution(6438237873518996908)
XLA Ops:
  10.1 46.2 %all-gather.13.cloned.1.call-done = bf16[1536,1024]{1,0:T(8,128)(2,1)} async-done(((bf16[1536,256]{1,0:T(8,128)(2,1)}), bf16[1536,1024]{1,0:T(8,128)(2,1)}) %all-gather.13.cloned.1.call-update) | async-done | bytes 3145744 | tf_op jit(solution)/shard_map/all_gather | solution.py:46
  60.6 22.7 %all-gather.15.cloned.1.call-done = bf16[3072,256]{1,0:T(8,128)(2,1)} async-done(((bf16[384,256]{1,0:T(8,128)(2,1)}), bf16[3072,256]{1,0:T(8,128)(2,1)}) %all-gather.15.cloned.1.call-update) | async-done | bytes 1572880 | tf_op jit(solution)/shard_map/all_gather | solution.py:50
  88.0 9.9 all_gather.50
  98.6 15.8 all_gather.51
  114.4 15.8 all_gather.52
  130.2 15.8 all_gather.53
  146.1 15.2 all_gather.54
  164.8 28.6 %all-gather.17.cloned.1.call-done = bf16[512,1024]{1,0:T(8,128)(2,1)} async-done(((bf16[512,256]{1,0:T(8,128)(2,1)}), bf16[512,1024]{1,0:T(8,128)(2,1)}) %all-gather.17.cloned.1.call-update) | async-done | bytes 1048592 | tf_op jit(solution)/shard_map/all_gather | solution.py:75
  197.5 6.0 fusion.42
  204.1 5.9 fusion.40
  215.3 5.9 convolution_convert_fusion
  223.1 5.8 convolution_convert_fusion.1
  232.0 61.1 %while.30 = (s32[]{:T(128)}, bf16[4,512,2,128]{3,1,2,0:T(8,128)(2,1)}, f32[4,2,512,1]{2,1,3,0:T(2,128)S(1)}, f32[4,2,512,1]{2,1,3,0:T(2,128)S(1)}, s32[4,512]{1,...) while((s32[]{:T(128)}, ...), condition=%wide.region_5.6_spmd.clone, body=%wide.region_2.5_spmd.clone.sunk | while | flops 1653081088 | bytes 56447168 | solution.py:124
  241.6 4.8 fusion.140
  256.8 4.8 fusion.140
  272.0 4.8 fusion.140
  287.3 4.8 fusion.140
  297.2 5.6 fusion.65
  303.6 10.7 fusion.78
  314.3 160.6 %all-reduce.4.cloned.1.call-done = f32[2048,1024]{1,0:T(8,128)} async-done(((f32[2048,1024]{1,0:T(8,128)}), f32[2048,1024]{1,0:T(8,128)}) %all-reduce.4.cloned.1.call-update) | async-done | bytes 8388624 | tf_op jit(solution)/shard_map/psum | solution.py:126
  474.9 5.5 fusion.77
  486.2 20.2 %all-gather.21.cloned.1.call-done = bf16[1024,1024]{1,0:T(8,128)(2,1)} async-done(((bf16[128,1024]{1,0:T(8,128)(2,1)}), bf16[1024,1024]{1,0:T(8,128)(2,1)}) %all-gather.21.cloned.1.call-update) | async-done | bytes 2097168 | tf_op jit(solution)/shard_map/all_gather | solution.py:54
  506.4 15.9 fusion.50
  524.3 7.0 fusion.79
  531.4 171.5 %all-reduce.8.cloned.1.call-done = f32[2048,1024]{1,0:T(8,128)} async-done(((f32[2048,1024]{1,0:T(8,128)}), f32[2048,1024]{1,0:T(8,128)}) %all-reduce.8.cloned.1.call-update) | async-done | bytes 8388624 | tf_op jit(solution)/shard_map/psum | solution.py:139
  702.9 8.2 multiply_reduce_fusion.1
  711.2 5.0 fusion.76
  726.1 122.1 %while.31 = (s32[]{:T(128)}, f32[3072,2,128]{0,2,1:T(8,128)S(1)}, f32[3072,2,128]{0,2,1:T(8,128)}, bf16[4,512,2,128]{3,1,2,0:T(8,128)(2,1)}, bf16[4,512,2,128]{3...) while((s32[]{:T(128)}, f32[3072,2,128]{0,2,1:T(8,128)S(1)}, ...), condition=%wide.region_15.16_spmd.clone, body=%wide.region_13.15_spmd.clone.sunk | while | flops 4066772992 | bytes 161038704 | solution.py:177
  729.0 7.8 fusion.148
  736.7 8.3 multiply_reduce_fusion.5
  745.1 5.7 multiply_convert_fusion.6
  759.4 7.8 fusion.148
  767.2 8.3 multiply_reduce_fusion.5
  775.5 5.7 multiply_convert_fusion.6
  789.9 7.8 fusion.148
  797.7 8.3 multiply_reduce_fusion.5
  806.0 5.7 multiply_convert_fusion.6
  820.4 7.8 fusion.148
  828.2 8.3 multiply_reduce_fusion.5
  836.5 5.7 multiply_convert_fusion.6
  858.5 4.6 slice_add_fusion
  863.1 11.8 pad_maximum_fusion
  876.5 12.2 convolution_convert_fusion.2
  888.7 423.9 %all-gather.27.cloned.1.call-done = f32[12288,1024]{1,0:T(8,128)} async-done(((f32[3072,1024]{1,0:T(8,128)}), f32[12288,1024]{1,0:T(8,128)}) %all-gather.27.cloned.1.call-update) | async-done | bytes 50331664 | tf_op jit(solution)/shard_map/all_gather | solution.py:193
  1312.7 24.8 %reduce_sum.127 = f32[3072,1024]{1,0:T(8,128)} reduce(f32[4,3072,1024]{2,1,0:T(8,128)} %bitcast.156, f32[]{:T(128)} %constant.78.clone.1), dimensions={0}, to_apply=%region_16.17 | reduce | flops 9437184 | bytes 62914564 | tf_op jit(solution)/shard_map/reduce_sum | solution.py:193
  1337.6 10.2 fusion.43
  1348.7 11.9 fusion.41
  1361.7 11.4 broadcast_add_fusion
  1373.1 5.0 copy-done.11
  1378.7 4.5 convolution_bitcast_fusion
  1383.4 10.0 fusion.83
  1393.5 13.0 fusion.74
  1406.5 5.8 fusion.59
  1412.6 4.9 fusion.51
  1417.5 5.7 fusion.81
  1423.3 5.6 fusion.82
  1438.8 14.3 reduce-scatter.25.cloned.1.call-done
  1454.6 39.1 %reduce-scatter.11.cloned.1.call-done = f32[384,256]{0,1:T(8,128)} async-done(((f32[3072,256]{0,1:T(8,128)}), f32[384,256]{0,1:T(8,128)}) %reduce-scatter.11.cloned.1.call-update) | async-done | bytes 393232 | tf_op jit(solution)/shard_map/reduce_scatter | solution.py:203
  1495.6 50.0 %reduce-scatter.21.cloned.1.call-done = f32[128,1024]{1,0:T(8,128)} async-done(((f32[1024,1024]{1,0:T(8,128)}), f32[128,1024]{1,0:T(8,128)}) %reduce-scatter.21.cloned.1.call-update) | async-done | bytes 524304 | tf_op jit(solution)/shard_map/reduce_scatter | solution.py:207
  1545.6 51.1 %reduce-scatter.23.cloned.1.call-done = f32[1024,128]{1,0:T(8,128)} async-done(((f32[1024,1024]{1,0:T(8,128)}), f32[1024,128]{1,0:T(8,128)}) %reduce-scatter.23.cloned.1.call-update) | async-done | bytes 524304 | tf_op jit(solution)/shard_map/reduce_scatter | solution.py:211
  1596.7 33.8 %reduce-scatter.19.cloned.1.call-done = f32[256,128]{1,0:T(8,128)} async-done(((f32[256,1024]{1,0:T(8,128)}), f32[256,128]{1,0:T(8,128)}) %reduce-scatter.19.cloned.1.call-update) | async-done | bytes 131088 | tf_op jit(solution)/shard_map/reduce_scatter | solution.py:210
  1630.5 33.6 %reduce-scatter.13.cloned.1.call-done = f32[128,256]{1,0:T(8,128)} async-done(((f32[1024,256]{1,0:T(8,128)}), f32[128,256]{1,0:T(8,128)}) %reduce-scatter.13.cloned.1.call-update) | async-done | bytes 131088 | tf_op jit(solution)/shard_map/reduce_scatter | solution.py:204
  1664.1 33.7 %reduce-scatter.15.cloned.1.call-done = f32[128,256]{1,0:T(8,128)} async-done(((f32[1024,256]{1,0:T(8,128)}), f32[128,256]{1,0:T(8,128)}) %reduce-scatter.15.cloned.1.call-update) | async-done | bytes 131088 | tf_op jit(solution)/shard_map/reduce_scatter | solution.py:205
  1697.7 33.5 %reduce-scatter.17.cloned.1.call-done = f32[128,256]{1,0:T(8,128)} async-done(((f32[1024,256]{1,0:T(8,128)}), f32[128,256]{1,0:T(8,128)}) %reduce-scatter.17.cloned.1.call-update) | async-done | bytes 131088 | tf_op jit(solution)/shard_map/reduce_scatter | solution.py:206
  (318 shorter events, 157.0 us)
Async XLA Ops:
  7.2 80.6 %copy-start.52 = (s32[1,4096]{1,0:T(1,128)S(1)}, s32[1,4096]{1,0:T(1,128)}, u32[]{:S(2)}) copy-start(s32[1,4096]{1,0:T(1,128)} %param.20) | copy-start | bytes 49156
  7.2 80.8 %copy-start.54 = (bf16[2,128]{1,0:T(2,128)(2,1)S(1)}, bf16[2,128]{1,0:T(2,128)(2,1)}, u32[]{:S(2)}) copy-start(bf16[2,128]{1,0:T(2,128)(2,1)} %param.21) | copy-start | bytes 1540
  7.2 91.4 %copy-start.47 = (bf16[128,256]{1,0:T(8,128)(2,1)S(1)}, bf16[128,256]{1,0:T(8,128)(2,1)}, u32[]{:S(2)}) copy-start(bf16[128,256]{1,0:T(8,128)(2,1)} %param.23) | copy-start | bytes 196612
  7.2 107.2 %copy-start.48 = (bf16[128,256]{1,0:T(8,128)(2,1)S(1)}, bf16[128,256]{1,0:T(8,128)(2,1)}, u32[]{:S(2)}) copy-start(bf16[128,256]{1,0:T(8,128)(2,1)} %param.24) | copy-start | bytes 196612
  7.2 49.1 %all-gather.13.cloned.1.call-start = ((), (), s32[]{:S(2)}) async-start(), calls=%async_computation.9 | async-start | bytes 3932160 | tf_op jit(solution)/shard_map/all_gather | solution.py:46
  8.0 122.3 %copy-start.49 = (bf16[128,256]{1,0:T(8,128)(2,1)S(1)}, bf16[128,256]{1,0:T(8,128)(2,1)}, u32[]{:S(2)}) copy-start(bf16[128,256]{1,0:T(8,128)(2,1)} %param.25) | copy-start | bytes 196612
  8.0 75.3 %all-gather.15.cloned.1.call-start = ((), (), s32[]{:S(2)}) async-start(), calls=%async_computation.10 | async-start | bytes 1769472 | tf_op jit(solution)/shard_map/all_gather | solution.py:50
  8.7 152.6 %all-gather.19.cloned.1.call-start = ((), (), s32[]{:S(2)}) async-start(), calls=%async_computation.12 | async-start | bytes 1310720 | tf_op jit(solution)/shard_map/all_gather | solution.py:45
  9.4 136.6 %copy-start.50 = (bf16[256,128]{1,0:T(8,128)(2,1)S(1)}, bf16[256,128]{1,0:T(8,128)(2,1)}, u32[]{:S(2)}) copy-start(bf16[256,128]{1,0:T(8,128)(2,1)} %param.26) | copy-start | bytes 196612
  9.5 155.3 %all-gather.11.cloned.1.call-start = ((), (), s32[]{:S(2)}) async-start(), calls=%async_computation.8 | async-start | bytes 5242880 | tf_op jit(solution)/shard_map/all_gather | solution.py:44
  10.0 183.4 %all-gather.17.cloned.1.call-start = ((), (), s32[]{:S(2)}) async-start(), calls=%async_computation.11 | async-start | bytes 1310720 | tf_op jit(solution)/shard_map/all_gather | solution.py:75
  60.5 100.8 %copy-start.19 = (bf16[512,3072]{1,0:T(8,128)(2,1)}, bf16[512,3072]{1,0:T(8,128)(2,1)S(1)}, u32[]{:S(2)}) copy-start(bf16[512,3072]{1,0:T(8,128)(2,1)S(1)} %reshape.251) | copy-start | bytes 9437188
  86.4 217.2 %all-gather.23.cloned.1.call-start = ((), (), s32[]{:S(2)}) async-start(), calls=%async_computation.15 | async-start | bytes 2359296 | tf_op jit(solution)/shard_map/all_gather | solution.py:58
  86.9 216.7 %all-gather.25.cloned.1.call-start = ((), (), s32[]{:S(2)}) async-start(), calls=%async_computation.17 | async-start | bytes 5242880 | tf_op jit(solution)/shard_map/all_gather | solution.py:47
  87.7 387.2 %all-reduce.4.cloned.1.call-start = ((), (), s32[]{:S(2)}) async-start(), calls=%async_computation.13 | async-start | bytes 16777216 | tf_op jit(solution)/shard_map/psum | solution.py:126
  98.5 111.4 %copy-start.45 = (f32[1,1024]{1,0:T(1,128)}, f32[1,1024]{1,0:T(1,128)S(1)}, u32[]{:S(2)}) copy-start(f32[1,1024]{1,0:T(1,128)S(1)} %get-tuple-element.379) | copy-start | bytes 12292
  161.3 42.7 %copy-start.12 = (bf16[512,1024]{1,0:T(8,128)(2,1)S(1)}, bf16[512,1024]{1,0:T(8,128)(2,1)}, u32[]{:S(2)}) copy-start(bf16[512,1024]{1,0:T(8,128)(2,1)} %all-gather.19.cloned.1.call-done) | copy-start | bytes 3145732
  193.4 10.7 copy-start.14
  197.5 6.0 copy-start.39
  197.5 15.1 copy-start.35
  215.3 7.8 copy-start.37
  293.1 9.7 copy-start.8
  293.1 9.7 copy-start.9
  302.8 203.6 %all-gather.21.cloned.1.call-start = ((), (), s32[]{:S(2)}) async-start(), calls=%async_computation.14 | async-start | bytes 2359296 | tf_op jit(solution)/shard_map/all_gather | solution.py:54
  303.5 399.3 %all-reduce.8.cloned.1.call-start = ((), (), s32[]{:S(2)}) async-start(), calls=%async_computation.18 | async-start | bytes 16777216 | tf_op jit(solution)/shard_map/psum | solution.py:139
  506.4 17.9 %copy-start.56 = (bf16[1024,1024]{1,0:T(8,128)(2,1)S(1)}, bf16[1024,1024]{1,0:T(8,128)(2,1)}, u32[]{:S(2)}) copy-start(bf16[1024,1024]{1,0:T(8,128)(2,1)} %all-gather.21.cloned.1.call-done) | copy-start | bytes 6291460
  531.3 781.4 %all-gather.27.cloned.1.call-start = ((), (), s32[]{:S(2)}) async-start(), calls=%async_computation.26 | async-start | bytes 62914560 | tf_op jit(solution)/shard_map/all_gather | solution.py:193
  702.9 8.2 copy-start.16
  711.1 5.0 copy-start.27
  716.2 4.4 copy-start.26
  726.1 10.7 copy-start.10
  726.1 10.7 copy-start.25
  745.0 5.7 copy-start.5
  756.5 10.7 copy-start.10
  756.5 10.7 copy-start.25
  775.5 5.7 copy-start.5
  787.0 10.7 copy-start.10
  787.0 10.7 copy-start.25
  806.0 5.7 copy-start.5
  817.5 10.7 copy-start.10
  817.5 10.7 copy-start.25
  836.5 5.7 copy-start.5
  874.9 554.0 %all-reduce.6.cloned.1.call-start = ((), (), s32[]{:S(2)}) async-start(), calls=%async_computation.16 | async-start | bytes 8388608 | tf_op jit(solution)/shard_map/psum | solution.py:132
  888.7 564.5 %reduce-scatter.25.cloned.1.call-start = ((), (), s32[]{:S(2)}) async-start(), calls=%async_computation.27 | async-start | bytes 589824
  1312.7 24.9 %copy-start.13 = (bf16[512,1024]{1,0:T(8,128)(2,1)S(1)}, bf16[512,1024]{1,0:T(8,128)(2,1)}, u32[]{:S(2)}) copy-start(bf16[512,1024]{1,0:T(8,128)(2,1)} %all-gather.19.cloned.1.call-done) | copy-start | bytes 3145732
  1312.7 24.9 %copy-start.15 = (bf16[512,1024]{1,0:T(8,128)(2,1)S(1)}, bf16[512,1024]{1,0:T(8,128)(2,1)}, u32[]{:S(2)}) copy-start(bf16[512,1024]{1,0:T(8,128)(2,1)} %all-gather.17.cloned.1.call-done) | copy-start | bytes 3145732
  1312.7 24.9 %copy-start.40 = (f32[3072]{0:T(1024)S(1)}, f32[3072]{0:T(1024)}, u32[]{:S(2)}) copy-start(f32[3072]{0:T(1024)} %copy-done.39) | copy-start | bytes 36868
  1312.7 24.9 %copy-start.46 = (f32[1,1024]{1,0:T(1,128)S(1)}, f32[1,1024]{1,0:T(1,128)}, u32[]{:S(2)}) copy-start(f32[1,1024]{1,0:T(1,128)} %copy-done.45) | copy-start | bytes 12292
  1337.5 10.3 copy-start.44
  1337.5 10.3 copy-start.2
  1337.6 11.2 copy-start.3
  1337.6 11.2 copy-start.42
  1348.7 11.9 copy-start.53
  1373.1 5.0 copy-start.11
  1378.3 115.4 %reduce-scatter.11.cloned.1.call-start = ((), (), s32[]{:S(2)}) async-start(), calls=%async_computation.19 | async-start | bytes 3538944 | tf_op jit(solution)/shard_map/reduce_scatter | solution.py:203
  1383.3 162.3 %reduce-scatter.21.cloned.1.call-start = ((), (), s32[]{:S(2)}) async-start(), calls=%async_computation.24 | async-start | bytes 4718592 | tf_op jit(solution)/shard_map/reduce_scatter | solution.py:207
  1393.4 13.1 copy-start.21
  1393.4 203.3 %reduce-scatter.23.cloned.1.call-start = ((), (), s32[]{:S(2)}) async-start(), calls=%async_computation.25 | async-start | bytes 4718592 | tf_op jit(solution)/shard_map/reduce_scatter | solution.py:211
  1406.4 224.1 %reduce-scatter.19.cloned.1.call-start = ((), (), s32[]{:S(2)}) async-start(), calls=%async_computation.23 | async-start | bytes 1179648 | tf_op jit(solution)/shard_map/reduce_scatter | solution.py:210
  1412.3 5.2 copy-start.23
  1412.3 251.7 %reduce-scatter.13.cloned.1.call-start = ((), (), s32[]{:S(2)}) async-start(), calls=%async_computation.20 | async-start | bytes 1179648 | tf_op jit(solution)/shard_map/reduce_scatter | solution.py:204
  1417.4 5.9 copy-start.18
  1417.5 280.3 %reduce-scatter.15.cloned.1.call-start = ((), (), s32[]{:S(2)}) async-start(), calls=%async_computation.21 | async-start | bytes 1179648 | tf_op jit(solution)/shard_map/reduce_scatter | solution.py:205
  1423.3 308.0 %reduce-scatter.17.cloned.1.call-start = ((), (), s32[]{:S(2)}) async-start(), calls=%async_computation.22 | async-start | bytes 1179648 | tf_op jit(solution)/shard_map/reduce_scatter | solution.py:206
  (39 other events, 97.5 us)
Sparse Core Ops, SparseCore 0:
  9.8 46.4 all-gather.12
  58.0 25.2 all-gather.14
  85.1 25.4 all-gather.18
  112.3 52.4 all-gather.10
  167.0 26.3 all-gather.16
  194.9 30.5 all-gather.22
  227.3 51.4 all-gather.24
  302.9 171.9 all-reduce.3
  476.5 29.8 all-gather.20
  531.4 171.4 all-reduce.7
  875.1 437.5 all-gather.26
  1315.8 103.5 all-reduce.5
  1421.7 31.3 reduce-scatter.24
  1455.3 38.3 reduce-scatter.10
  1496.4 49.1 reduce-scatter.20
  1548.3 48.3 reduce-scatter.22
  1599.4 31.0 reduce-scatter.18
  1633.2 30.8 reduce-scatter.12
  1666.9 30.7 reduce-scatter.14
  1700.4 30.7 reduce-scatter.16
